TPU v7x, 128 devices: a whole 4x4x4 slice. The times are simulated.
128 devices in a mesh: grp: 16 (over x, y_lo, core), blk: 8 (over z, y_hi).
Axes of the slice: x: 4, y: 4 (y_hi: 2, y_lo: 2; y = y_hi * 2 + y_lo), z: 4, core: 2. Of those that a mesh axis runs over, the one named last changes fastest.
Arguments:
- nodes: float32 [16, 3, 128, 256], P('grp', None, 'blk'), may hold values from -4 to 4
- panels: float32 [16, 3, 4096], P('grp', None, 'blk'), may hold values from -4 to 4
- nu_field: float32 [16, 128, 256], P('grp', 'blk'), may hold values from 0.2 to 1.5
- vorticity: float32 [16, 128, 256], P('grp', 'blk'), may hold values from 1 to 100
- flow: float32 [16, 4, 128, 256], P('grp', None, 'blk'), may hold values from -6 to 6
- fringe_block: int32 [16384], P(('grp', 'blk')), may hold values from 0 to 31
- fringe_size: int32 [16384], P(('grp', 'blk')), may hold values from 1 to 128
- fringe_owner: int32 [16384, 1], P(('grp', 'blk')), may hold values from 0 to 127; in each aligned block of 128 rows (0 to 127, 128 to 255, ...) at most 2 rows name the same one
- fringe_cell: int32 [16384], P(('grp', 'blk')), may hold values from 0 to 15
Outputs:
- wall_distance: float32 [16, 128, 256], P('grp', 'blk')
- nu_next: float32 [16, 128, 256], P('grp', 'blk')
- offbody: float32 [2048, 5, 128], P(('grp', 'blk'))
Inputs may be any that keep to these rules, and one draw needn't show every extreme that they name: `fringe_owner`: among the 128 slots of one device, at most 2 name the same owner device.
All inputs are finite; a program needn't handle non-finite values.
Results may differ from a plain program's by a relative error of at most 0.00012.
Values sent between devices are 32-bit elements; how exact they have to be, the bound alone decides.
No kernel may reach another device: no remote copies, remote signals or barrier semaphores. Data moves between devices by JAX's collectives and lax.ppermute only.
A program may use at most 64 MiB of HBM per device.

v0:
```python
import math
import jax
import jax.numpy as jnp
from jax import lax
from jax.sharding import PartitionSpec as P

BLOCK = 128
VARS = 5
CAP = 2
OB = 16


def padded_2(cells, sides, width):
    for axis, dim in sides:
        count = lax.axis_size(axis)
        head = lax.slice_in_dim(cells, 0, width, axis=dim)
        tail = lax.slice_in_dim(cells, cells.shape[dim] - width, cells.shape[dim], axis=dim)
        cells = jnp.concatenate(
            [
                lax.ppermute(tail, axis, [(i, (i + 1) % count) for i in range(count)]),
                cells,
                lax.ppermute(head, axis, [((i + 1) % count, i) for i in range(count)]),
            ],
            axis=dim,
        )
    return cells


def sa_step(nu_ext, dist, vort):
    centre = nu_ext[1:-1]
    east = nu_ext[2:]
    west = nu_ext[:-2]
    padded = jnp.pad(centre, ((0, 0), (1, 1)))
    north = padded[:, 2:]
    south = padded[:, :-2]
    flux = (1.0 + 0.5 * (centre + east)) * (east - centre) - (1.0 + 0.5 * (centre + west)) * (
        centre - west
    )
    flux = (
        flux
        + (1.0 + 0.5 * (centre + north)) * (north - centre)
        - (1.0 + 0.5 * (centre + south)) * (centre - south)
    )
    grads = 0.25 * ((east - west) * (east - west) + (north - south) * (north - south))
    diffusion = (flux + 0.622 * grads) / (2.0 / 3.0)
    ratio = centre / dist
    return centre + 0.02 * (0.1355 * vort * centre - 3.24 * ratio * ratio + diffusion)


def per_device(
    nodes, panels, nu_field, vorticity, flow, fringe_block, fringe_size, fringe_owner, fringe_cell
):
    lines = nodes.shape[2]
    points_j = nodes.shape[3]
    points = nodes[0].reshape(3, -1)
    init = jnp.full((points.shape[1],), 1e30, jnp.float32)
    piece = lax.all_gather(panels[0], "blk", axis=1, tiled=True)
    count = piece.shape[1]
    width = math.gcd(count, 256)
    blocks = jnp.transpose(piece.reshape(3, count // width, width), (1, 0, 2))

    def visit(carry, panel_block):
        delta0 = points[0][:, None] - panel_block[0][None, :]
        delta1 = points[1][:, None] - panel_block[1][None, :]
        delta2 = points[2][:, None] - panel_block[2][None, :]
        dsq = delta0 * delta0 + delta1 * delta1 + delta2 * delta2
        return (jnp.minimum(carry, jnp.min(dsq, axis=1)), None)

    result, unused = lax.scan(visit, init, blocks)
    dist = jnp.sqrt(result + 0.25).reshape(lines, points_j)
    vort = vorticity[0]
    nu_now = nu_field[0]
    for step in range(2):
        ext = padded_2(nu_now, (("blk", 0),), 1)
        nu_now = sa_step(ext, dist, vort)
    state = jnp.concatenate([nu_now[None], flow[0]], axis=0)
    state = state.reshape(VARS, lines * (points_j // BLOCK), BLOCK)
    values = jnp.transpose(jnp.take(state, fringe_block, axis=1), (1, 0, 2))
    live = (jnp.arange(BLOCK, dtype=jnp.int32)[None, :] < fringe_size[:, None]).astype(jnp.float32)
    values = values * live[:, None, :]
    group_count = lax.axis_size("grp")
    member_count = lax.axis_size("blk")
    devices_all = group_count * member_count
    dest = fringe_owner[:, 0]
    hits = (dest[:, None] == jnp.arange(devices_all, dtype=jnp.int32)[None, :]).astype(jnp.int32)
    rank = jnp.sum((jnp.cumsum(hits, axis=0) - hits) * hits, axis=1)
    slot = dest * CAP + rank
    buffer = jnp.zeros((devices_all * CAP, VARS, BLOCK), jnp.float32).at[slot].set(values)
    cells = (
        jnp.zeros((devices_all * CAP,), jnp.float32).at[slot].set(fringe_cell.astype(jnp.float32))
    )
    got_values, got_cells = (
        lax.all_to_all(
            buffer.reshape(devices_all, CAP, VARS, BLOCK),
            ("grp", "blk"),
            split_axis=0,
            concat_axis=0,
            tiled=True,
        ),
        lax.all_to_all(
            cells.reshape(devices_all, CAP), ("grp", "blk"), split_axis=0, concat_axis=0, tiled=True
        ),
    )
    rows = got_values.reshape(devices_all * CAP, VARS * BLOCK)
    flat_cells = got_cells.reshape(devices_all * CAP)
    select = (flat_cells[None, :] == jnp.arange(OB, dtype=jnp.float32)[:, None]).astype(jnp.float32)
    offbody = jnp.dot(
        select, rows, precision=lax.Precision.HIGHEST, preferred_element_type=jnp.float32
    )
    return (dist[None], nu_now[None], offbody.reshape(OB, VARS, BLOCK))


def solution(mesh):
    in_specs = (
        P("grp", None, "blk", None),
        P("grp", None, "blk"),
        P("grp", "blk", None),
        P("grp", "blk", None),
        P("grp", None, "blk", None),
        P(("grp", "blk")),
        P(("grp", "blk")),
        P(("grp", "blk"), None),
        P(("grp", "blk")),
    )
    out_specs = (P("grp", "blk", None), P("grp", "blk", None), P(("grp", "blk"), None, None))
    return jax.shard_map(
        per_device, mesh=mesh, in_specs=in_specs, out_specs=out_specs, check_vma=False
    )
```

profile of v0, /device:TPU:1, one launch (start us, length us, event | category | flops | bytes accessed | tf_op | source)
XLA Modules:
  0.0 139.1 jit_solution(15647237432715452222)
XLA Ops:
  0.6 0.7 slice_bitcast_fusion.1
  1.4 7.2 %collective-permute-start = (f32[1,256]{1,0:T(1,128)S(1)}, f32[1,256]{1,0:T(1,128)S(1)}, u32[]{:S(2)}, u32[]{:S(2)}) collective-permute-start(f32[1,256]{1,0:T(1,128)S(1)} %get-tuple-element.73), channel_id=1, source_target_pairs={{1,0},{2,1},{3,2},{4,3},{5,4},{6,5},{7,6},{0,7},{9,8},{10,9},{11,1... | collective-permute-start | bytes 3080 | tf_op jit(solution)/shard_map/ppermute | solution.py:22
  8.6 0.7 fusion
  9.3 0.2 reduce_window_sum.11
  9.5 0.8 select_reduce_fusion
  10.3 0.7 fusion.52
  11.0 0.7 convert_element_type.18
  11.6 1.0 scatter_custom_fusion
  12.6 0.8 all_to_all.9
  13.4 9.9 %all-to-all-start = ((f32[128,1,2]{2,1,0:T(1,128)}), f32[128,1,2]{2,1,0:T(1,128)S(1)}, u32[]{:S(2)}, u32[]{:S(2)}) async-start(f32[128,1,2]{2,1,0:T(1,128)} %bitcast.9), calls=%async_computation | async-start | bytes 131072 | tf_op jit(solution)/shard_map/all_to_all | solution.py:100
  23.3 26.8 %all-gather = f32[1,3,4096]{2,0,1:T(1,128)S(1)} all-gather(f32[1,3,512]{2,0,1:T(1,128)} %param.12), channel_id=2, replica_groups=mesh['grp'=16,'blk'=8] {'blk'}, dimensions={2}, use_global_device_ids=true | all-gather | bytes 55296 | tf_op jit(solution)/shard_map/all_gather | solution.py:57
  50.2 0.1 reduce
  50.3 0.8 copy.41
  51.1 43.5 %while.11 = (s32[]{:T(128)}, f32[4096]{0:T(1024)S(1)}, f32[3,4096]{1,0:T(4,128)S(1)}, f32[16,3,256]{2,0,1:T(8,128)S(1)}, s32[]{:T(128)}, /*index=5*/s32[]{:T(128)}, s32[]{}, s32[]{}) while((s32[]{:T(128)}, f32[4096]{0:T(1024)S(1)}, f32[3,4096]{1,0:T(4,128)S(1)}, f32[16,3,256]{2,0,1:T(8,128)S(1)}, s32[]{:T(128)}, ...), condition=%wide.region_2.3_spmd.clone, body=%wide.region_0.2_spmd.clone.sunk | while | flops 9441285 | bytes 222339 | solution.py:69
  51.2 2.6 %add_reduce_fusion.2 = f32[4096]{0:T(1024)S(1)} fusion(f32[256]{0:T(256)S(1)} %bitcast.82, f32[4096]{0:T(1024)S(1)} %bitcast.76, f32[256]{0:T(256)S(1)} %bitcast.81, f32[4096]{0:T(1024)S(1)} %bitcast.77, f32[256]{0:T(256)S(1)} %bitcast.80, f32[4096]{0:T(1024)S(1)} %bitcast.75), kind=kLoop, calls=%fused_computation.3.clone.1 | loop fusion | flops 9433088 | bytes 68608 | tf_op jit(solution)/shard_map/while/body/eval_jaxpr/reduce_min | solution.py:67
  53.9 2.6 %add_reduce_fusion.2 = f32[4096]{0:T(1024)S(1)} fusion(f32[256]{0:T(256)S(1)} %bitcast.82, f32[4096]{0:T(1024)S(1)} %bitcast.76, f32[256]{0:T(256)S(1)} %bitcast.81, f32[4096]{0:T(1024)S(1)} %bitcast.77, f32[256]{0:T(256)S(1)} %bitcast.80, f32[4096]{0:T(1024)S(1)} %bitcast.75), kind=kLoop, calls=%fused_computation.3.clone.1 | loop fusion | flops 9433088 | bytes 68608 | tf_op jit(solution)/shard_map/while/body/eval_jaxpr/reduce_min | solution.py:67
  56.7 2.6 %add_reduce_fusion.2 = f32[4096]{0:T(1024)S(1)} fusion(f32[256]{0:T(256)S(1)} %bitcast.82, f32[4096]{0:T(1024)S(1)} %bitcast.76, f32[256]{0:T(256)S(1)} %bitcast.81, f32[4096]{0:T(1024)S(1)} %bitcast.77, f32[256]{0:T(256)S(1)} %bitcast.80, f32[4096]{0:T(1024)S(1)} %bitcast.75), kind=kLoop, calls=%fused_computation.3.clone.1 | loop fusion | flops 9433088 | bytes 68608 | tf_op jit(solution)/shard_map/while/body/eval_jaxpr/reduce_min | solution.py:67
  59.4 2.6 %add_reduce_fusion.2 = f32[4096]{0:T(1024)S(1)} fusion(f32[256]{0:T(256)S(1)} %bitcast.82, f32[4096]{0:T(1024)S(1)} %bitcast.76, f32[256]{0:T(256)S(1)} %bitcast.81, f32[4096]{0:T(1024)S(1)} %bitcast.77, f32[256]{0:T(256)S(1)} %bitcast.80, f32[4096]{0:T(1024)S(1)} %bitcast.75), kind=kLoop, calls=%fused_computation.3.clone.1 | loop fusion | flops 9433088 | bytes 68608 | tf_op jit(solution)/shard_map/while/body/eval_jaxpr/reduce_min | solution.py:67
  62.1 2.6 %add_reduce_fusion.2 = f32[4096]{0:T(1024)S(1)} fusion(f32[256]{0:T(256)S(1)} %bitcast.82, f32[4096]{0:T(1024)S(1)} %bitcast.76, f32[256]{0:T(256)S(1)} %bitcast.81, f32[4096]{0:T(1024)S(1)} %bitcast.77, f32[256]{0:T(256)S(1)} %bitcast.80, f32[4096]{0:T(1024)S(1)} %bitcast.75), kind=kLoop, calls=%fused_computation.3.clone.1 | loop fusion | flops 9433088 | bytes 68608 | tf_op jit(solution)/shard_map/while/body/eval_jaxpr/reduce_min | solution.py:67
  64.8 2.6 %add_reduce_fusion.2 = f32[4096]{0:T(1024)S(1)} fusion(f32[256]{0:T(256)S(1)} %bitcast.82, f32[4096]{0:T(1024)S(1)} %bitcast.76, f32[256]{0:T(256)S(1)} %bitcast.81, f32[4096]{0:T(1024)S(1)} %bitcast.77, f32[256]{0:T(256)S(1)} %bitcast.80, f32[4096]{0:T(1024)S(1)} %bitcast.75), kind=kLoop, calls=%fused_computation.3.clone.1 | loop fusion | flops 9433088 | bytes 68608 | tf_op jit(solution)/shard_map/while/body/eval_jaxpr/reduce_min | solution.py:67
  67.5 2.6 %add_reduce_fusion.2 = f32[4096]{0:T(1024)S(1)} fusion(f32[256]{0:T(256)S(1)} %bitcast.82, f32[4096]{0:T(1024)S(1)} %bitcast.76, f32[256]{0:T(256)S(1)} %bitcast.81, f32[4096]{0:T(1024)S(1)} %bitcast.77, f32[256]{0:T(256)S(1)} %bitcast.80, f32[4096]{0:T(1024)S(1)} %bitcast.75), kind=kLoop, calls=%fused_computation.3.clone.1 | loop fusion | flops 9433088 | bytes 68608 | tf_op jit(solution)/shard_map/while/body/eval_jaxpr/reduce_min | solution.py:67
  70.3 2.6 %add_reduce_fusion.2 = f32[4096]{0:T(1024)S(1)} fusion(f32[256]{0:T(256)S(1)} %bitcast.82, f32[4096]{0:T(1024)S(1)} %bitcast.76, f32[256]{0:T(256)S(1)} %bitcast.81, f32[4096]{0:T(1024)S(1)} %bitcast.77, f32[256]{0:T(256)S(1)} %bitcast.80, f32[4096]{0:T(1024)S(1)} %bitcast.75), kind=kLoop, calls=%fused_computation.3.clone.1 | loop fusion | flops 9433088 | bytes 68608 | tf_op jit(solution)/shard_map/while/body/eval_jaxpr/reduce_min | solution.py:67
  73.0 2.6 %add_reduce_fusion.2 = f32[4096]{0:T(1024)S(1)} fusion(f32[256]{0:T(256)S(1)} %bitcast.82, f32[4096]{0:T(1024)S(1)} %bitcast.76, f32[256]{0:T(256)S(1)} %bitcast.81, f32[4096]{0:T(1024)S(1)} %bitcast.77, f32[256]{0:T(256)S(1)} %bitcast.80, f32[4096]{0:T(1024)S(1)} %bitcast.75), kind=kLoop, calls=%fused_computation.3.clone.1 | loop fusion | flops 9433088 | bytes 68608 | tf_op jit(solution)/shard_map/while/body/eval_jaxpr/reduce_min | solution.py:67
  75.7 2.6 %add_reduce_fusion.2 = f32[4096]{0:T(1024)S(1)} fusion(f32[256]{0:T(256)S(1)} %bitcast.82, f32[4096]{0:T(1024)S(1)} %bitcast.76, f32[256]{0:T(256)S(1)} %bitcast.81, f32[4096]{0:T(1024)S(1)} %bitcast.77, f32[256]{0:T(256)S(1)} %bitcast.80, f32[4096]{0:T(1024)S(1)} %bitcast.75), kind=kLoop, calls=%fused_computation.3.clone.1 | loop fusion | flops 9433088 | bytes 68608 | tf_op jit(solution)/shard_map/while/body/eval_jaxpr/reduce_min | solution.py:67
  78.4 2.6 %add_reduce_fusion.2 = f32[4096]{0:T(1024)S(1)} fusion(f32[256]{0:T(256)S(1)} %bitcast.82, f32[4096]{0:T(1024)S(1)} %bitcast.76, f32[256]{0:T(256)S(1)} %bitcast.81, f32[4096]{0:T(1024)S(1)} %bitcast.77, f32[256]{0:T(256)S(1)} %bitcast.80, f32[4096]{0:T(1024)S(1)} %bitcast.75), kind=kLoop, calls=%fused_computation.3.clone.1 | loop fusion | flops 9433088 | bytes 68608 | tf_op jit(solution)/shard_map/while/body/eval_jaxpr/reduce_min | solution.py:67
  81.1 2.6 %add_reduce_fusion.2 = f32[4096]{0:T(1024)S(1)} fusion(f32[256]{0:T(256)S(1)} %bitcast.82, f32[4096]{0:T(1024)S(1)} %bitcast.76, f32[256]{0:T(256)S(1)} %bitcast.81, f32[4096]{0:T(1024)S(1)} %bitcast.77, f32[256]{0:T(256)S(1)} %bitcast.80, f32[4096]{0:T(1024)S(1)} %bitcast.75), kind=kLoop, calls=%fused_computation.3.clone.1 | loop fusion | flops 9433088 | bytes 68608 | tf_op jit(solution)/shard_map/while/body/eval_jaxpr/reduce_min | solution.py:67
  83.9 2.6 %add_reduce_fusion.2 = f32[4096]{0:T(1024)S(1)} fusion(f32[256]{0:T(256)S(1)} %bitcast.82, f32[4096]{0:T(1024)S(1)} %bitcast.76, f32[256]{0:T(256)S(1)} %bitcast.81, f32[4096]{0:T(1024)S(1)} %bitcast.77, f32[256]{0:T(256)S(1)} %bitcast.80, f32[4096]{0:T(1024)S(1)} %bitcast.75), kind=kLoop, calls=%fused_computation.3.clone.1 | loop fusion | flops 9433088 | bytes 68608 | tf_op jit(solution)/shard_map/while/body/eval_jaxpr/reduce_min | solution.py:67
  86.6 2.6 %add_reduce_fusion.2 = f32[4096]{0:T(1024)S(1)} fusion(f32[256]{0:T(256)S(1)} %bitcast.82, f32[4096]{0:T(1024)S(1)} %bitcast.76, f32[256]{0:T(256)S(1)} %bitcast.81, f32[4096]{0:T(1024)S(1)} %bitcast.77, f32[256]{0:T(256)S(1)} %bitcast.80, f32[4096]{0:T(1024)S(1)} %bitcast.75), kind=kLoop, calls=%fused_computation.3.clone.1 | loop fusion | flops 9433088 | bytes 68608 | tf_op jit(solution)/shard_map/while/body/eval_jaxpr/reduce_min | solution.py:67
  89.3 2.6 %add_reduce_fusion.2 = f32[4096]{0:T(1024)S(1)} fusion(f32[256]{0:T(256)S(1)} %bitcast.82, f32[4096]{0:T(1024)S(1)} %bitcast.76, f32[256]{0:T(256)S(1)} %bitcast.81, f32[4096]{0:T(1024)S(1)} %bitcast.77, f32[256]{0:T(256)S(1)} %bitcast.80, f32[4096]{0:T(1024)S(1)} %bitcast.75), kind=kLoop, calls=%fused_computation.3.clone.1 | loop fusion | flops 9433088 | bytes 68608 | tf_op jit(solution)/shard_map/while/body/eval_jaxpr/reduce_min | solution.py:67
  92.0 2.6 %add_reduce_fusion.2 = f32[4096]{0:T(1024)S(1)} fusion(f32[256]{0:T(256)S(1)} %bitcast.82, f32[4096]{0:T(1024)S(1)} %bitcast.76, f32[256]{0:T(256)S(1)} %bitcast.81, f32[4096]{0:T(1024)S(1)} %bitcast.77, f32[256]{0:T(256)S(1)} %bitcast.80, f32[4096]{0:T(1024)S(1)} %bitcast.75), kind=kLoop, calls=%fused_computation.3.clone.1 | loop fusion | flops 9433088 | bytes 68608 | tf_op jit(solution)/shard_map/while/body/eval_jaxpr/reduce_min | solution.py:67
  94.9 0.1 fusion.5
  95.0 3.5 %collective-permute-start.2 = (f32[1,256]{1,0:T(1,128)S(1)}, f32[1,256]{1,0:T(1,128)S(1)}, u32[]{:S(2)}, u32[]{:S(2)}) collective-permute-start(f32[1,256]{1,0:T(1,128)S(1)} %get-tuple-element.71), channel_id=1, source_target_pairs={{1,0},{2,1},{3,2},{4,3},{5,4},{6,5},{7,6},{0,7},{9,8},{10,9},{11,1... | collective-permute-start | bytes 3080 | tf_op jit(solution)/shard_map/ppermute | solution.py:22
  98.6 0.6 collective-permute-done.2
  99.2 5.3 %collective-permute-done.3 = f32[1,256]{1,0:T(1,128)S(1)} collective-permute-done((f32[1,256]{1,0:T(1,128)S(1)}, f32[1,256]{1,0:T(1,128)S(1)}, u32[]{:S(2)}, u32[]{:S(2)}) %collective-permute-start.3) | collective-permute-done | bytes 1056 | tf_op jit(solution)/shard_map/ppermute | solution.py:20
  104.7 0.8 gather_fusion
  105.5 0.2 select_multiply_fusion
  105.8 4.3 %scatter_fusion = f32[256,5,128]{2,1,0:T(8,128)S(1)} fusion(f32[256,5,128]{2,1,0:T(8,128)S(1)} %broadcast_in_dim.35, s32[128]{0:T(128)S(1)} %fusion.52, f32[128,5,128]{2,1,0:T(8,128)S(1)} %select_multiply_fusion), kind=kCustom, calls=%fused_computation.2 | custom fusion | bytes 983552 | tf_op jit(solution)/shard_map/scatter | solution.py:88
  110.1 1.2 copy.32
  111.3 10.9 %all-to-all-start.1 = ((f32[128,2,5,128]{3,1,2,0:T(2,128)}), f32[128,2,5,128]{3,1,2,0:T(2,128)S(1)}, u32[]{:S(2)}, u32[]{:S(2)}) async-start(f32[128,2,5,128]{3,1,2,0:T(2,128)} %copy.32), calls=%async_computation.1 | async-start | bytes 1310720 | tf_op jit(solution)/shard_map/all_to_all | solution.py:93
  122.2 0.6 broadcast_in_dim_reshape.4
  122.8 0.5 broadcast.112
  123.3 0.8 reduce.4
  124.1 0.1 eq.36
  124.3 13.3 %all-to-all-done.1 = f32[128,2,5,128]{3,1,2,0:T(2,128)S(1)} async-done(((f32[128,2,5,128]{3,1,2,0:T(2,128)}), f32[128,2,5,128]{3,1,2,0:T(2,128)S(1)}, u32[]{:S(2)}, u32[]{:S(2)}) %all-to-all-start.1) | async-done | bytes 655392 | tf_op jit(solution)/shard_map/all_to_all | solution.py:93
  137.6 0.1 copy.33
  137.7 0.1 copy.46
  137.8 0.2 copy.34
  138.1 1.0 fusion.49
  (80 shorter events, 1.4 us)
Async XLA Ops:
  1.4 93.5 %collective-permute-start = (f32[1,256]{1,0:T(1,128)S(1)}, f32[1,256]{1,0:T(1,128)S(1)}, u32[]{:S(2)}, u32[]{:S(2)}) collective-permute-start(f32[1,256]{1,0:T(1,128)S(1)} %get-tuple-element.73), channel_id=1, source_target_pairs={{1,0},{2,1},{3,2},{4,3},{5,4},{6,5},{7,6},{0,7},{9,8},{10,9},{11,1... | collective-permute-start | bytes 3080 | tf_op jit(solution)/shard_map/ppermute | solution.py:22
  8.6 86.3 %collective-permute-start.1 = (f32[1,256]{1,0:T(1,128)S(1)}, f32[1,256]{1,0:T(1,128)S(1)}, u32[]{:S(2)}, u32[]{:S(2)}) collective-permute-start(f32[1,256]{1,0:T(1,128)S(1)} %get-tuple-element.74), channel_id=1, source_target_pairs={{0,1},{1,2},{2,3},{3,4},{4,5},{5,6},{6,7},{7,0},{8,9},{9,10},{10,1... | collective-permute-start | bytes 3080 | tf_op jit(solution)/shard_map/ppermute | solution.py:20
  12.6 82.1 %copy-start.5 = (s32[128]{0:T(128)S(1)}, s32[128]{0:T(128)}, u32[]{:S(2)}) copy-start(s32[128]{0:T(128)} %param.16) | copy-start | bytes 1540
  12.6 82.1 %copy-start.4 = (s32[128]{0:T(128)S(1)}, s32[128]{0:T(128)}, u32[]{:S(2)}) copy-start(s32[128]{0:T(128)} %param.17) | copy-start | bytes 1540
  13.4 81.5 %copy-start.2 = (f32[1,16,256]{2,1,0:T(8,128)S(1)}, f32[1,16,256]{2,1,0:T(8,128)}, u32[]{:S(2)}) copy-start(f32[1,16,256]{2,1,0:T(8,128)} %param.14) | copy-start | bytes 49156
  13.4 81.5 %copy-start.3 = (f32[1,16,256]{2,1,0:T(8,128)S(1)}, f32[1,16,256]{2,1,0:T(8,128)}, u32[]{:S(2)}) copy-start(f32[1,16,256]{2,1,0:T(8,128)} %param.13) | copy-start | bytes 49156
  13.4 97.9 %all-to-all-start = ((f32[128,1,2]{2,1,0:T(1,128)}), f32[128,1,2]{2,1,0:T(1,128)S(1)}, u32[]{:S(2)}, u32[]{:S(2)}) async-start(f32[128,1,2]{2,1,0:T(1,128)} %bitcast.9), calls=%async_computation | async-start | bytes 131072 | tf_op jit(solution)/shard_map/all_to_all | solution.py:100
  23.3 75.2 %copy-start = (f32[1,4,16,256]{3,2,1,0:T(8,128)S(1)}, f32[1,4,16,256]{3,2,1,0:T(8,128)}, u32[]{:S(2)}) copy-start(f32[1,4,16,256]{3,2,1,0:T(8,128)} %param.15) | copy-start | bytes 196612
  95.0 4.3 %collective-permute-start.2 = (f32[1,256]{1,0:T(1,128)S(1)}, f32[1,256]{1,0:T(1,128)S(1)}, u32[]{:S(2)}, u32[]{:S(2)}) collective-permute-start(f32[1,256]{1,0:T(1,128)S(1)} %get-tuple-element.71), channel_id=1, source_target_pairs={{1,0},{2,1},{3,2},{4,3},{5,4},{6,5},{7,6},{0,7},{9,8},{10,9},{11,1... | collective-permute-start | bytes 3080 | tf_op jit(solution)/shard_map/ppermute | solution.py:22
  98.5 6.0 %collective-permute-start.3 = (f32[1,256]{1,0:T(1,128)S(1)}, f32[1,256]{1,0:T(1,128)S(1)}, u32[]{:S(2)}, u32[]{:S(2)}) collective-permute-start(f32[1,256]{1,0:T(1,128)S(1)} %get-tuple-element.72), channel_id=1, source_target_pairs={{0,1},{1,2},{2,3},{3,4},{4,5},{5,6},{6,7},{7,0},{8,9},{9,10},{10,1... | collective-permute-start | bytes 3080 | tf_op jit(solution)/shard_map/ppermute | solution.py:20
  104.6 1.1 copy-start.1
  111.3 26.3 %all-to-all-start.1 = ((f32[128,2,5,128]{3,1,2,0:T(2,128)}), f32[128,2,5,128]{3,1,2,0:T(2,128)S(1)}, u32[]{:S(2)}, u32[]{:S(2)}) async-start(f32[128,2,5,128]{3,1,2,0:T(2,128)} %copy.32), calls=%async_computation.1 | async-start | bytes 1310720 | tf_op jit(solution)/shard_map/all_to_all | solution.py:93
where the time goes:
time: 140 us; the launch traced here: 139 us
  other arithmetic  46.4 us (33%)
  starting transfers between devices  31.6 us (23%)
  blocking collectives  26.8 us (19%)
  waiting for transfers between devices  19.3 us (14%)
  local copies, waits for them, and re-layouts  12.3 us (9%)
    reduce_min x16, other arithmetic, visit(): return (jnp.minimum(carry, jnp.min(dsq, axis=1)), None)  41.7 us
    all_gather x1, blocking collectives, per_device(): piece = lax.all_gather(panels[0], 'blk', axis=1, tiled=True)  26.8 us
    all_to_all x1, waiting for transfers between devices, per_device(): lax.all_to_all(buffer.reshape(devices_all, CAP, VARS, BLOCK), ('grp', 'bl...  13.3 us
    all_to_all x1, starting transfers between devices, per_device(): lax.all_to_all(buffer.reshape(devices_all, CAP, VARS, BLOCK), ('grp', 'bl...  10.9 us
    ppermute x2, starting transfers between devices, padded_2(): lax.ppermute(head, axis, [((i + 1) % count, i) for i in range(count)])  10.7 us
    all_to_all x1, starting transfers between devices, per_device(): lax.all_to_all(cells.reshape(devices_all, CAP), ('grp', 'blk'), split_axi...  9.92 us
    ppermute x2, waiting for transfers between devices, padded_2(): lax.ppermute(tail, axis, [(i, (i + 1) % count) for i in range(count)])  5.31 us
    scatter x1, local copies, waits for them, and re-layouts, per_device(): jnp.zeros((devices_all * CAP, VARS, BLOCK), jnp.float32).at[slot]  4.3 us
  transfers between devices with their start and end apart: 6, of which 3 were waited for; matrix products, arithmetic and copies ran while one was open for 41% of the time, Pallas kernels for 0%

commit v1 on v0

--- a/solution.py
+++ b/solution.py
@@ -54,7 +54,18 @@
     points_j = nodes.shape[3]
     points = nodes[0].reshape(3, -1)
     init = jnp.full((points.shape[1],), 1e30, jnp.float32)
-    piece = lax.all_gather(panels[0], "blk", axis=1, tiled=True)
+
+    def cut_sizes(chunk):
+        new = lax.all_to_all(
+            jnp.stack([chunk for _ in range(lax.axis_size("blk"))], axis=0),
+            axis_name="blk",
+            split_axis=0,
+            concat_axis=0,
+        )
+        q_next = jnp.concatenate(new, 1)
+        return q_next
+
+    piece = cut_sizes(panels[0])
     count = piece.shape[1]
     width = math.gcd(count, 256)
     blocks = jnp.transpose(piece.reshape(3, count // width, width), (1, 0, 2))

time: 140 us -> 120 us (0.86)
  blocking collectives: 26.8 us -> 0 us
  starting transfers between devices: 31.6 us -> 35.6 us
  other arithmetic: 46.4 us -> 48.2 us
    all_gather x1 -> x0, blocking collectives: 26.8 us -> none  [per_device(): piece = lax.all_gather(panels[0], 'blk', axis=1, tiled=True)]
    all_to_all x0 -> x1, starting transfers between devices: none -> 8.48 us  [cut_sizes(): lax.all_to_all(jnp.stack([chunk for _ in range(lax.axis_size('blk'))], ax...]
    all_to_all x1, starting transfers between devices: 10.9 us -> 5.75 us  [per_device(): lax.all_to_all(buffer.reshape(devices_all, CAP, VARS, BLOCK), ('grp', 'bl...]
  transfers between devices with their start and end apart: 6 -> 7, of which waited for: 3 -> 3; matrix products, arithmetic and copies ran while one was open for 41% -> 50% of each run, Pallas kernels for 0% -> 0%
where the time goes in v1:
time: 120 us; the launch traced here: 119 us
  other arithmetic  48.2 us (40%)
  starting transfers between devices  35.6 us (30%)
  waiting for transfers between devices  19.3 us (16%)
  local copies, waits for them, and re-layouts  13.6 us (11%)
    reduce_min x16, other arithmetic, visit(): return (jnp.minimum(carry, jnp.min(dsq, axis=1)), None)  41.7 us
    all_to_all x1, waiting for transfers between devices, per_device(): lax.all_to_all(buffer.reshape(devices_all, CAP, VARS, BLOCK), ('grp', 'bl...  13.3 us
    ppermute x2, starting transfers between devices, padded_2(): lax.ppermute(head, axis, [((i + 1) % count, i) for i in range(count)])  10.9 us
    all_to_all x1, starting transfers between devices, per_device(): lax.all_to_all(cells.reshape(devices_all, CAP), ('grp', 'blk'), split_axi...  10.5 us
    all_to_all x1, starting transfers between devices, cut_sizes(): lax.all_to_all(jnp.stack([chunk for _ in range(lax.axis_size('blk'))], ax...  8.48 us
    all_to_all x1, starting transfers between devices, per_device(): lax.all_to_all(buffer.reshape(devices_all, CAP, VARS, BLOCK), ('grp', 'bl...  5.75 us
    ppermute x2, waiting for transfers between devices, padded_2(): lax.ppermute(tail, axis, [(i, (i + 1) % count) for i in range(count)])  5.31 us
    scatter x1, local copies, waits for them, and re-layouts, per_device(): jnp.zeros((devices_all * CAP, VARS, BLOCK), jnp.float32).at[slot]  4.3 us
  transfers between devices with their start and end apart: 7, of which 3 were waited for; matrix products, arithmetic and copies ran while one was open for 50% of the time, Pallas kernels for 0%

profile of v1, /device:TPU:1, one launch (start us, length us, event | category | flops | bytes accessed | tf_op | source)
XLA Modules:
  0.0 119.4 jit_solution(11892178275012597096)
XLA Ops:
  0.6 0.7 copy.39
  1.3 0.6 stack.3
  2.0 8.5 %all-to-all-start = ((f32[8,3,512]{2,1,0:T(4,128)}), f32[8,3,512]{2,1,0:T(4,128)S(1)}, u32[]{:S(2)}, u32[]{:S(2)}) async-start(f32[8,3,512]{2,1,0:T(4,128)} %stack.3), calls=%async_computation | async-start | bytes 131072 | tf_op jit(solution)/shard_map/all_to_all | solution.py:59
  10.4 0.7 slice_bitcast_fusion.1
  11.2 5.1 %collective-permute-start = (f32[1,256]{1,0:T(1,128)S(1)}, f32[1,256]{1,0:T(1,128)S(1)}, u32[]{:S(2)}, u32[]{:S(2)}) collective-permute-start(f32[1,256]{1,0:T(1,128)S(1)} %get-tuple-element.57), channel_id=1, source_target_pairs={{1,0},{2,1},{3,2},{4,3},{5,4},{6,5},{7,6},{0,7},{9,8},{10,9},{11,1... | collective-permute-start | bytes 3080 | tf_op jit(solution)/shard_map/ppermute | solution.py:22
  16.2 0.7 compare_select_fusion
  16.9 0.7 fusion.1
  17.7 0.7 fusion
  18.4 0.2 reduce_window_sum.11
  18.6 0.8 select_reduce_fusion
  19.4 0.7 fusion.52
  20.1 0.7 compare_and_fusion
  20.8 0.8 copy.34
  21.6 0.7 convert_element_type.18
  22.3 1.0 scatter_custom_fusion
  23.2 0.8 all_to_all.13
  24.0 10.5 %all-to-all-start.1 = ((f32[128,1,2]{2,1,0:T(1,128)}), f32[128,1,2]{2,1,0:T(1,128)S(1)}, u32[]{:S(2)}, u32[]{:S(2)}) async-start(f32[128,1,2]{2,1,0:T(1,128)} %bitcast.11), calls=%async_computation.1 | async-start | bytes 131072 | tf_op jit(solution)/shard_map/all_to_all | solution.py:111
  34.5 43.4 %while.11 = (s32[]{:T(128)}, f32[4096]{0:T(1024)S(1)}, f32[3,4096]{1,0:T(4,128)S(1)}, f32[16,3,256]{2,1,0:T(4,128)S(1)}, s32[]{:T(128)}, /*index=5*/s32[]{:T(128)}, s32[]{}, s32[]{}) while((s32[]{:T(128)}, f32[4096]{0:T(1024)S(1)}, f32[3,4096]{1,0:T(4,128)S(1)}, f32[16,3,256]{2,1,0:T(4,128)S(1)}, s32[]{:T(128)}, ...), condition=%wide.region_2.3_spmd.clone, body=%wide.region_0.2_spmd.clone.sunk | while | flops 9441285 | bytes 222339 | solution.py:80
  34.6 2.6 %add_reduce_fusion.2 = f32[4096]{0:T(1024)S(1)} fusion(f32[256]{0:T(256)S(1)} %bitcast.76, f32[4096]{0:T(1024)S(1)} %bitcast.71, f32[256]{0:T(256)S(1)} %bitcast.75, f32[4096]{0:T(1024)S(1)} %bitcast.72, f32[256]{0:T(256)S(1)} %bitcast.74, f32[4096]{0:T(1024)S(1)} %bitcast.70), kind=kLoop, calls=%fused_computation.3.clone.1 | loop fusion | flops 9433088 | bytes 68608 | tf_op jit(solution)/shard_map/while/body/eval_jaxpr/reduce_min | solution.py:78
  37.3 2.6 %add_reduce_fusion.2 = f32[4096]{0:T(1024)S(1)} fusion(f32[256]{0:T(256)S(1)} %bitcast.76, f32[4096]{0:T(1024)S(1)} %bitcast.71, f32[256]{0:T(256)S(1)} %bitcast.75, f32[4096]{0:T(1024)S(1)} %bitcast.72, f32[256]{0:T(256)S(1)} %bitcast.74, f32[4096]{0:T(1024)S(1)} %bitcast.70), kind=kLoop, calls=%fused_computation.3.clone.1 | loop fusion | flops 9433088 | bytes 68608 | tf_op jit(solution)/shard_map/while/body/eval_jaxpr/reduce_min | solution.py:78
  40.0 2.6 %add_reduce_fusion.2 = f32[4096]{0:T(1024)S(1)} fusion(f32[256]{0:T(256)S(1)} %bitcast.76, f32[4096]{0:T(1024)S(1)} %bitcast.71, f32[256]{0:T(256)S(1)} %bitcast.75, f32[4096]{0:T(1024)S(1)} %bitcast.72, f32[256]{0:T(256)S(1)} %bitcast.74, f32[4096]{0:T(1024)S(1)} %bitcast.70), kind=kLoop, calls=%fused_computation.3.clone.1 | loop fusion | flops 9433088 | bytes 68608 | tf_op jit(solution)/shard_map/while/body/eval_jaxpr/reduce_min | solution.py:78
  42.7 2.6 %add_reduce_fusion.2 = f32[4096]{0:T(1024)S(1)} fusion(f32[256]{0:T(256)S(1)} %bitcast.76, f32[4096]{0:T(1024)S(1)} %bitcast.71, f32[256]{0:T(256)S(1)} %bitcast.75, f32[4096]{0:T(1024)S(1)} %bitcast.72, f32[256]{0:T(256)S(1)} %bitcast.74, f32[4096]{0:T(1024)S(1)} %bitcast.70), kind=kLoop, calls=%fused_computation.3.clone.1 | loop fusion | flops 9433088 | bytes 68608 | tf_op jit(solution)/shard_map/while/body/eval_jaxpr/reduce_min | solution.py:78
  45.4 2.6 %add_reduce_fusion.2 = f32[4096]{0:T(1024)S(1)} fusion(f32[256]{0:T(256)S(1)} %bitcast.76, f32[4096]{0:T(1024)S(1)} %bitcast.71, f32[256]{0:T(256)S(1)} %bitcast.75, f32[4096]{0:T(1024)S(1)} %bitcast.72, f32[256]{0:T(256)S(1)} %bitcast.74, f32[4096]{0:T(1024)S(1)} %bitcast.70), kind=kLoop, calls=%fused_computation.3.clone.1 | loop fusion | flops 9433088 | bytes 68608 | tf_op jit(solution)/shard_map/while/body/eval_jaxpr/reduce_min | solution.py:78
  48.1 2.6 %add_reduce_fusion.2 = f32[4096]{0:T(1024)S(1)} fusion(f32[256]{0:T(256)S(1)} %bitcast.76, f32[4096]{0:T(1024)S(1)} %bitcast.71, f32[256]{0:T(256)S(1)} %bitcast.75, f32[4096]{0:T(1024)S(1)} %bitcast.72, f32[256]{0:T(256)S(1)} %bitcast.74, f32[4096]{0:T(1024)S(1)} %bitcast.70), kind=kLoop, calls=%fused_computation.3.clone.1 | loop fusion | flops 9433088 | bytes 68608 | tf_op jit(solution)/shard_map/while/body/eval_jaxpr/reduce_min | solution.py:78
  50.8 2.6 %add_reduce_fusion.2 = f32[4096]{0:T(1024)S(1)} fusion(f32[256]{0:T(256)S(1)} %bitcast.76, f32[4096]{0:T(1024)S(1)} %bitcast.71, f32[256]{0:T(256)S(1)} %bitcast.75, f32[4096]{0:T(1024)S(1)} %bitcast.72, f32[256]{0:T(256)S(1)} %bitcast.74, f32[4096]{0:T(1024)S(1)} %bitcast.70), kind=kLoop, calls=%fused_computation.3.clone.1 | loop fusion | flops 9433088 | bytes 68608 | tf_op jit(solution)/shard_map/while/body/eval_jaxpr/reduce_min | solution.py:78
  53.6 2.6 %add_reduce_fusion.2 = f32[4096]{0:T(1024)S(1)} fusion(f32[256]{0:T(256)S(1)} %bitcast.76, f32[4096]{0:T(1024)S(1)} %bitcast.71, f32[256]{0:T(256)S(1)} %bitcast.75, f32[4096]{0:T(1024)S(1)} %bitcast.72, f32[256]{0:T(256)S(1)} %bitcast.74, f32[4096]{0:T(1024)S(1)} %bitcast.70), kind=kLoop, calls=%fused_computation.3.clone.1 | loop fusion | flops 9433088 | bytes 68608 | tf_op jit(solution)/shard_map/while/body/eval_jaxpr/reduce_min | solution.py:78
  56.3 2.6 %add_reduce_fusion.2 = f32[4096]{0:T(1024)S(1)} fusion(f32[256]{0:T(256)S(1)} %bitcast.76, f32[4096]{0:T(1024)S(1)} %bitcast.71, f32[256]{0:T(256)S(1)} %bitcast.75, f32[4096]{0:T(1024)S(1)} %bitcast.72, f32[256]{0:T(256)S(1)} %bitcast.74, f32[4096]{0:T(1024)S(1)} %bitcast.70), kind=kLoop, calls=%fused_computation.3.clone.1 | loop fusion | flops 9433088 | bytes 68608 | tf_op jit(solution)/shard_map/while/body/eval_jaxpr/reduce_min | solution.py:78
  59.0 2.6 %add_reduce_fusion.2 = f32[4096]{0:T(1024)S(1)} fusion(f32[256]{0:T(256)S(1)} %bitcast.76, f32[4096]{0:T(1024)S(1)} %bitcast.71, f32[256]{0:T(256)S(1)} %bitcast.75, f32[4096]{0:T(1024)S(1)} %bitcast.72, f32[256]{0:T(256)S(1)} %bitcast.74, f32[4096]{0:T(1024)S(1)} %bitcast.70), kind=kLoop, calls=%fused_computation.3.clone.1 | loop fusion | flops 9433088 | bytes 68608 | tf_op jit(solution)/shard_map/while/body/eval_jaxpr/reduce_min | solution.py:78
  61.7 2.6 %add_reduce_fusion.2 = f32[4096]{0:T(1024)S(1)} fusion(f32[256]{0:T(256)S(1)} %bitcast.76, f32[4096]{0:T(1024)S(1)} %bitcast.71, f32[256]{0:T(256)S(1)} %bitcast.75, f32[4096]{0:T(1024)S(1)} %bitcast.72, f32[256]{0:T(256)S(1)} %bitcast.74, f32[4096]{0:T(1024)S(1)} %bitcast.70), kind=kLoop, calls=%fused_computation.3.clone.1 | loop fusion | flops 9433088 | bytes 68608 | tf_op jit(solution)/shard_map/while/body/eval_jaxpr/reduce_min | solution.py:78
  64.4 2.6 %add_reduce_fusion.2 = f32[4096]{0:T(1024)S(1)} fusion(f32[256]{0:T(256)S(1)} %bitcast.76, f32[4096]{0:T(1024)S(1)} %bitcast.71, f32[256]{0:T(256)S(1)} %bitcast.75, f32[4096]{0:T(1024)S(1)} %bitcast.72, f32[256]{0:T(256)S(1)} %bitcast.74, f32[4096]{0:T(1024)S(1)} %bitcast.70), kind=kLoop, calls=%fused_computation.3.clone.1 | loop fusion | flops 9433088 | bytes 68608 | tf_op jit(solution)/shard_map/while/body/eval_jaxpr/reduce_min | solution.py:78
  67.1 2.6 %add_reduce_fusion.2 = f32[4096]{0:T(1024)S(1)} fusion(f32[256]{0:T(256)S(1)} %bitcast.76, f32[4096]{0:T(1024)S(1)} %bitcast.71, f32[256]{0:T(256)S(1)} %bitcast.75, f32[4096]{0:T(1024)S(1)} %bitcast.72, f32[256]{0:T(256)S(1)} %bitcast.74, f32[4096]{0:T(1024)S(1)} %bitcast.70), kind=kLoop, calls=%fused_computation.3.clone.1 | loop fusion | flops 9433088 | bytes 68608 | tf_op jit(solution)/shard_map/while/body/eval_jaxpr/reduce_min | solution.py:78
  69.8 2.6 %add_reduce_fusion.2 = f32[4096]{0:T(1024)S(1)} fusion(f32[256]{0:T(256)S(1)} %bitcast.76, f32[4096]{0:T(1024)S(1)} %bitcast.71, f32[256]{0:T(256)S(1)} %bitcast.75, f32[4096]{0:T(1024)S(1)} %bitcast.72, f32[256]{0:T(256)S(1)} %bitcast.74, f32[4096]{0:T(1024)S(1)} %bitcast.70), kind=kLoop, calls=%fused_computation.3.clone.1 | loop fusion | flops 9433088 | bytes 68608 | tf_op jit(solution)/shard_map/while/body/eval_jaxpr/reduce_min | solution.py:78
  72.6 2.6 %add_reduce_fusion.2 = f32[4096]{0:T(1024)S(1)} fusion(f32[256]{0:T(256)S(1)} %bitcast.76, f32[4096]{0:T(1024)S(1)} %bitcast.71, f32[256]{0:T(256)S(1)} %bitcast.75, f32[4096]{0:T(1024)S(1)} %bitcast.72, f32[256]{0:T(256)S(1)} %bitcast.74, f32[4096]{0:T(1024)S(1)} %bitcast.70), kind=kLoop, calls=%fused_computation.3.clone.1 | loop fusion | flops 9433088 | bytes 68608 | tf_op jit(solution)/shard_map/while/body/eval_jaxpr/reduce_min | solution.py:78
  75.3 2.6 %add_reduce_fusion.2 = f32[4096]{0:T(1024)S(1)} fusion(f32[256]{0:T(256)S(1)} %bitcast.76, f32[4096]{0:T(1024)S(1)} %bitcast.71, f32[256]{0:T(256)S(1)} %bitcast.75, f32[4096]{0:T(1024)S(1)} %bitcast.72, f32[256]{0:T(256)S(1)} %bitcast.74, f32[4096]{0:T(1024)S(1)} %bitcast.70), kind=kLoop, calls=%fused_computation.3.clone.1 | loop fusion | flops 9433088 | bytes 68608 | tf_op jit(solution)/shard_map/while/body/eval_jaxpr/reduce_min | solution.py:78
  78.1 5.8 %collective-permute-start.2 = (f32[1,256]{1,0:T(1,128)S(1)}, f32[1,256]{1,0:T(1,128)S(1)}, u32[]{:S(2)}, u32[]{:S(2)}) collective-permute-start(f32[1,256]{1,0:T(1,128)S(1)} %get-tuple-element.55), channel_id=1, source_target_pairs={{1,0},{2,1},{3,2},{4,3},{5,4},{6,5},{7,6},{0,7},{9,8},{10,9},{11,1... | collective-permute-start | bytes 3080 | tf_op jit(solution)/shard_map/ppermute | solution.py:22
  84.0 0.6 collective-permute-done.2
  84.7 5.3 %collective-permute-done.3 = f32[1,256]{1,0:T(1,128)S(1)} collective-permute-done((f32[1,256]{1,0:T(1,128)S(1)}, f32[1,256]{1,0:T(1,128)S(1)}, u32[]{:S(2)}, u32[]{:S(2)}) %collective-permute-start.3) | collective-permute-done | bytes 1056 | tf_op jit(solution)/shard_map/ppermute | solution.py:20
  90.2 0.8 gather_fusion
  90.9 0.2 select_multiply_fusion
  91.2 4.3 %scatter_fusion = f32[256,5,128]{2,1,0:T(8,128)S(1)} fusion(f32[256,5,128]{2,1,0:T(8,128)S(1)} %broadcast_in_dim.35, s32[128]{0:T(128)S(1)} %fusion.52, f32[128,5,128]{2,1,0:T(8,128)S(1)} %select_multiply_fusion), kind=kCustom, calls=%fused_computation.2 | custom fusion | bytes 983552 | tf_op jit(solution)/shard_map/scatter | solution.py:99
  95.5 1.2 copy.28
  96.7 5.7 %all-to-all-start.2 = ((f32[128,2,5,128]{3,1,2,0:T(2,128)}), f32[128,2,5,128]{3,1,2,0:T(2,128)S(1)}, u32[]{:S(2)}, u32[]{:S(2)}) async-start(f32[128,2,5,128]{3,1,2,0:T(2,128)} %copy.28), calls=%async_computation.2 | async-start | bytes 1310720 | tf_op jit(solution)/shard_map/all_to_all | solution.py:104
  102.5 0.5 broadcast.112
  103.0 0.8 reduce.3
  103.9 0.6 broadcast_in_dim_reshape.4
  104.5 13.3 %all-to-all-done.2 = f32[128,2,5,128]{3,1,2,0:T(2,128)S(1)} async-done(((f32[128,2,5,128]{3,1,2,0:T(2,128)}), f32[128,2,5,128]{3,1,2,0:T(2,128)S(1)}, u32[]{:S(2)}, u32[]{:S(2)}) %all-to-all-start.2) | async-done | bytes 655392 | tf_op jit(solution)/shard_map/all_to_all | solution.py:104
  118.1 0.2 copy.30
  118.3 1.0 fusion.49
  (77 shorter events, 1.7 us)
Async XLA Ops:
  2.0 22.0 %all-to-all-start = ((f32[8,3,512]{2,1,0:T(4,128)}), f32[8,3,512]{2,1,0:T(4,128)S(1)}, u32[]{:S(2)}, u32[]{:S(2)}) async-start(f32[8,3,512]{2,1,0:T(4,128)} %stack.3), calls=%async_computation | async-start | bytes 131072 | tf_op jit(solution)/shard_map/all_to_all | solution.py:59
  11.2 66.8 %collective-permute-start = (f32[1,256]{1,0:T(1,128)S(1)}, f32[1,256]{1,0:T(1,128)S(1)}, u32[]{:S(2)}, u32[]{:S(2)}) collective-permute-start(f32[1,256]{1,0:T(1,128)S(1)} %get-tuple-element.57), channel_id=1, source_target_pairs={{1,0},{2,1},{3,2},{4,3},{5,4},{6,5},{7,6},{0,7},{9,8},{10,9},{11,1... | collective-permute-start | bytes 3080 | tf_op jit(solution)/shard_map/ppermute | solution.py:22
  16.2 61.7 %collective-permute-start.1 = (f32[1,256]{1,0:T(1,128)S(1)}, f32[1,256]{1,0:T(1,128)S(1)}, u32[]{:S(2)}, u32[]{:S(2)}) collective-permute-start(f32[1,256]{1,0:T(1,128)S(1)} %get-tuple-element.58), channel_id=1, source_target_pairs={{0,1},{1,2},{2,3},{3,4},{4,5},{5,6},{6,7},{7,0},{8,9},{9,10},{10,1... | collective-permute-start | bytes 3080 | tf_op jit(solution)/shard_map/ppermute | solution.py:20
  17.6 60.3 %copy-start.2 = (f32[1,16,256]{2,1,0:T(8,128)S(1)}, f32[1,16,256]{2,1,0:T(8,128)}, u32[]{:S(2)}) copy-start(f32[1,16,256]{2,1,0:T(8,128)} %param.14) | copy-start | bytes 49156
  17.6 60.3 %copy-start.3 = (f32[1,16,256]{2,1,0:T(8,128)S(1)}, f32[1,16,256]{2,1,0:T(8,128)}, u32[]{:S(2)}) copy-start(f32[1,16,256]{2,1,0:T(8,128)} %param.13) | copy-start | bytes 49156
  18.4 65.5 %copy-start = (f32[1,4,16,256]{3,2,1,0:T(8,128)S(1)}, f32[1,4,16,256]{3,2,1,0:T(8,128)}, u32[]{:S(2)}) copy-start(f32[1,4,16,256]{3,2,1,0:T(8,128)} %param.15) | copy-start | bytes 196612
  24.0 72.7 %all-to-all-start.1 = ((f32[128,1,2]{2,1,0:T(1,128)}), f32[128,1,2]{2,1,0:T(1,128)S(1)}, u32[]{:S(2)}, u32[]{:S(2)}) async-start(f32[128,1,2]{2,1,0:T(1,128)} %bitcast.11), calls=%async_computation.1 | async-start | bytes 131072 | tf_op jit(solution)/shard_map/all_to_all | solution.py:111
  78.1 6.6 %collective-permute-start.2 = (f32[1,256]{1,0:T(1,128)S(1)}, f32[1,256]{1,0:T(1,128)S(1)}, u32[]{:S(2)}, u32[]{:S(2)}) collective-permute-start(f32[1,256]{1,0:T(1,128)S(1)} %get-tuple-element.55), channel_id=1, source_target_pairs={{1,0},{2,1},{3,2},{4,3},{5,4},{6,5},{7,6},{0,7},{9,8},{10,9},{11,1... | collective-permute-start | bytes 3080 | tf_op jit(solution)/shard_map/ppermute | solution.py:22
  83.9 6.0 %collective-permute-start.3 = (f32[1,256]{1,0:T(1,128)S(1)}, f32[1,256]{1,0:T(1,128)S(1)}, u32[]{:S(2)}, u32[]{:S(2)}) collective-permute-start(f32[1,256]{1,0:T(1,128)S(1)} %get-tuple-element.56), channel_id=1, source_target_pairs={{0,1},{1,2},{2,3},{3,4},{4,5},{5,6},{6,7},{7,0},{8,9},{9,10},{10,1... | collective-permute-start | bytes 3080 | tf_op jit(solution)/shard_map/ppermute | solution.py:20
  90.1 1.1 copy-start.1
  96.7 21.1 %all-to-all-start.2 = ((f32[128,2,5,128]{3,1,2,0:T(2,128)}), f32[128,2,5,128]{3,1,2,0:T(2,128)S(1)}, u32[]{:S(2)}, u32[]{:S(2)}) async-start(f32[128,2,5,128]{3,1,2,0:T(2,128)} %copy.28), calls=%async_computation.2 | async-start | bytes 1310720 | tf_op jit(solution)/shard_map/all_to_all | solution.py:104
